TPU v7x, 32 devices: a whole 2x2x4 slice. The times are simulated.
32 devices in a mesh: tok: 8 (over z, x), tp: 4 (over y, core).
Axes of the slice: x: 2, y: 2, z: 4, core: 2. Of those that a mesh axis runs over, the one named last changes fastest.
Arguments:
- tokens: bfloat16 [36928, 768], P('tok'), may hold values from -6 to 6
- slot_index: int32 [36928], P('tok'), may hold values from -1 to 18477, as said below
- segment: int32 [36928], P('tok'), may hold values from 0 to 3, as said below
- router: float32 [768], replicated, may hold values from -0.21875 to 0.21875
- first_norm: float32 [2, 768], replicated, may hold values from -0.6 to 1.3
- qkv_weight: bfloat16 [768, 3, 768], P(None, None, 'tp'), may hold values from -0.21875 to 0.21875
- qv_bias: float32 [2, 768], P(None, 'tp'), may hold values from -4 to 4
- out_weight: bfloat16 [768, 768], P('tp'), may hold values from -1.75 to 1.75
- out_bias: float32 [768], P('tp'), may hold values from -4 to 4
- second_norm: float32 [2, 768], replicated, may hold values from -0.6 to 1.3
- up_weight: bfloat16 [768, 3072], P(None, 'tp'), may hold values from -0.21875 to 0.21875
- up_bias: float32 [3072], P('tp'), may hold values from -4 to 4
- down_weight: bfloat16 [3072, 768], P('tp'), may hold values from -0.109375 to 0.109375
- down_bias: float32 [768], P('tp'), may hold values from -4 to 4
- cotangent: bfloat16 [36928, 768], P('tok'), may hold values from -6 to 6
Outputs:
- layer_out: bfloat16 [36928, 768], P('tok', 'tp')
- d_tokens: float32 [36928, 768], P('tok', 'tp')
- d_qkv_weight: float32 [768, 3, 768], P(None, None, 'tp')
- d_qv_bias: float32 [2, 768], P(None, 'tp')
- d_out_weight: float32 [768, 768], P('tp')
- d_out_bias: float32 [768], P('tp')
- d_up_weight: float32 [768, 3072], P(None, 'tp')
- d_up_bias: float32 [3072], P('tp')
- d_down_weight: float32 [3072, 768], P('tp')
- d_down_bias: float32 [768], P('tp')
- d_first_norm: float32 [2, 768], P(None, 'tp')
- d_second_norm: float32 [2, 768], P(None, 'tp')
- d_router: float32 [768], P('tp')
Inputs may be any that keep to these rules, and one draw needn't show every extreme that they name: `slot_index`: -1 where the router leaves a patch out; else a slot of the compact buffers, slot // 289 being its row buffer, owned by index slot // 2312 of tok. No slot is named twice, each buffer's named slots are its lowest ones, every index of tok holds exactly 2168 selected patches and owns 2168 named slots, and at most 271 of the selected patches of one index of tok lie in rows of one owner. `segment`: within a row buffer the segments of named slots never fall from one slot to the next.
All inputs are finite; a program needn't handle non-finite values.
Results may differ from a plain program's by a relative error of at most 0.013.
Values may be sent and summed in bfloat16 or wider, within the bound.
No kernel may reach another device: no remote copies, remote signals or barrier semaphores. Data moves between devices by JAX's collectives and lax.ppermute only.
A program may use at most 320 MiB of HBM per device.

v0:
```python
import jax
import jax.numpy as jnp
from jax import lax
from jax.sharding import PartitionSpec as P

HD = 64
ROWS_DEV = 8
SLOTS = 289
EPSILON = 1e-06
MASKED_SCORE = -1000000000.0
BF = jnp.bfloat16
F32 = jnp.float32
EXACT = lax.Precision.HIGHEST


def ceil_to(value, step):
    return -(-value // step) * step


def normal_parts(values):
    row_mean = jnp.mean(values, axis=-1, keepdims=True)
    centered = values - row_mean
    inverse = lax.rsqrt(jnp.mean(centered * centered, axis=-1, keepdims=True) + EPSILON)
    return (centered * inverse, inverse)


def norm_back(grad_in, normal, inverse, gain_row):
    scaled = grad_in * gain_row
    return inverse * (
        scaled
        - jnp.mean(scaled, axis=-1, keepdims=True)
        - normal * jnp.mean(scaled * normal, axis=-1, keepdims=True)
    )


def mul(left, right):
    return lax.dot_general(left, right, (((1,), (0,)), ((), ())), preferred_element_type=F32)


def mul_t0(left, right):
    return lax.dot_general(left, right, (((0,), (0,)), ((), ())), preferred_element_type=F32)


def mul_t1(left, right):
    return lax.dot_general(left, right, (((1,), (1,)), ((), ())), preferred_element_type=F32)


def hot(rows, cols):
    return (rows[:, None] == cols[None, :]).astype(BF)


def columns_of(source, part, shares):
    width = source.shape[-1] // shares
    return lax.dynamic_slice_in_dim(source, part * width, width, source.ndim - 1)


def body(
    tokens,
    slot_index,
    segment,
    router,
    first_norm,
    qkv_weight,
    qv_bias,
    out_weight,
    out_bias,
    second_norm,
    up_weight,
    up_bias,
    down_weight,
    down_bias,
    cotangent,
):
    peers = lax.axis_size("tok")
    shares = lax.axis_size("tp")
    part = lax.axis_index("tp")
    half_bit = part % 2
    pair_bit = part // 2
    half_swap = [(i, i ^ 1) for i in range(shares)]
    pair_swap = [(i, i ^ 2) for i in range(shares)]
    count, width = tokens.shape
    inner = qkv_weight.shape[2]
    heads_local = inner // HD
    owned = ROWS_DEV * SLOTS
    live = owned - owned // 16
    capacity = -(-live // peers)
    quarter = -(-capacity // shares)
    block = ceil_to(quarter + 1, 8)
    picked = peers * block
    idle_share = -(-(count - live) // shares)
    idle = ceil_to(idle_share, 16)
    own = picked + idle
    chosen = slot_index >= 0
    owner = jnp.where(chosen, slot_index // owned, peers)
    lanes = jnp.arange(peers, dtype=jnp.int32)
    match = (owner[:, None] == lanes[None, :]).astype(jnp.int32)
    rank = jnp.sum(jnp.cumsum(match, axis=0) * match, axis=1) - 1
    idle_rank = jnp.cumsum(jnp.where(chosen, 0, 1)) - 1
    piece = rank // quarter
    offset = rank % quarter
    mine = chosen & (piece % 2 == half_bit)
    far = piece // 2 ^ pair_bit
    send_row = jnp.where(mine, (owner * 2 + far) * block + offset, -1)
    picked_row = jnp.where(mine & (far == 0), owner * block + offset, -1)
    own_row = jnp.where(
        chosen,
        picked_row,
        jnp.where(idle_rank // idle_share == part, picked + idle_rank % idle_share, -1),
    )
    back_picked = jnp.where(chosen, piece * picked + owner * block + offset, -1)
    back_idle = jnp.where(chosen, -1, idle_rank // idle_share * idle + idle_rank % idle_share)
    up_all = lax.all_gather(up_weight, "tp")
    down_all = lax.all_gather(down_weight, "tp")
    send_hot = hot(jnp.arange(2 * picked, dtype=jnp.int32), send_row)
    own_hot = hot(jnp.arange(own, dtype=jnp.int32), own_row)
    send_in = mul(send_hot, tokens)
    send_hat, _ = normal_parts(send_in)
    send_rows = (send_hat * first_norm[0] + first_norm[1]).astype(BF)
    local_slot = jnp.where(chosen, slot_index % owned, 0)
    marks = jnp.stack([local_slot // 64 + 1, local_slot % 64, segment])
    block_of = jnp.where(mine, owner * 2 + far, -1)
    block_hot = jnp.arange(2 * peers, dtype=jnp.int32)[:, None] == block_of[None, :]
    mark_left = jnp.where(block_hot[None], marks[:, None, :], 0).astype(BF)
    mark_right = hot(offset, jnp.arange(128, dtype=jnp.int32))
    mark_rows = mul(mark_left.reshape(6 * peers, count), mark_right).astype(BF)
    mark_rows = mark_rows.reshape(3, 2 * peers, 128).transpose(1, 0, 2).reshape(2 * peers, 1, 384)
    mark_rows = jnp.pad(mark_rows, ((0, 0), (0, 0), (0, width - 384)))
    row_kind = jnp.arange(block, dtype=jnp.int32)[None, :, None] == quarter
    send_rows = jnp.where(row_kind, mark_rows, send_rows.reshape(2 * peers, block, width))
    got_near = lax.all_to_all(
        send_rows.reshape(peers, 2, block, width), "tok", split_axis=0, concat_axis=0, tiled=True
    )
    got_far = lax.ppermute(got_near, "tp", half_swap)
    got = jnp.stack([got_near, got_far])
    mark = got[:, :, :, quarter, :].astype(jnp.int32)
    recv_slot = (mark[..., 0:block] - 1) * 64 + mark[..., 128 : 128 + block]
    recv_segment = mark[..., 256 : 256 + block]
    slot_rows = recv_slot.transpose(0, 2, 1, 3).reshape(4 * picked)
    segment_rows = recv_segment.transpose(0, 2, 1, 3).reshape(4 * picked)
    features = got.transpose(0, 2, 1, 3, 4).reshape(4 * picked, width)
    pad = 304
    ids = jnp.arange(ROWS_DEV * pad, dtype=jnp.int32)
    slot_ids = jnp.where(ids % pad < SLOTS, ids // pad * SLOTS + ids % pad, -1000)
    slot_hot = hot(slot_ids, slot_rows)
    slot_features = mul(slot_hot, features).astype(BF)
    flat_weight = qkv_weight.reshape(width, 3 * inner)
    bias_row = jnp.concatenate([qv_bias[0], jnp.zeros_like(qv_bias[0]), qv_bias[1]])
    slot_qkv = (mul(slot_features, flat_weight) + bias_row).astype(BF)
    slot_segment = (
        jnp.sum(jnp.where(slot_hot > 0, segment_rows[None, :] + 1, 0), axis=1) - 1
    ).reshape(ROWS_DEV, pad)
    allowed = (slot_segment[:, :, None] == slot_segment[:, None, :]) & (
        slot_segment[:, None, :] >= 0
    )
    grouped = slot_qkv.reshape(ROWS_DEV, pad, 3, heads_local, HD)
    query, key, value = (grouped[:, :, 0], grouped[:, :, 1], grouped[:, :, 2])
    score_scale = HD ** (-0.5)
    scores = jnp.einsum("rqhe,rkhe->rhqk", query, key, preferred_element_type=F32) * score_scale
    scores = jnp.where(allowed[:, None], scores, MASKED_SCORE)
    top = jnp.max(scores, axis=-1, keepdims=True)
    raised = jnp.exp(scores - top)
    weights = raised / jnp.sum(raised, axis=-1, keepdims=True)
    weights_low = weights.astype(BF)
    attended = jnp.einsum("rhqk,rkhe->rqhe", weights_low, value, preferred_element_type=F32)
    heads = attended.reshape(ROWS_DEV * pad, inner).astype(BF)
    heads_rows = mul_t0(slot_hot, heads).astype(BF)
    bias_full = lax.dynamic_update_slice(
        jnp.zeros((width,), F32), out_bias, (part * (width // shares),)
    )

    def share_sum(partial):
        near, far_half = (partial[: 2 * picked], partial[2 * picked :])
        got_half = lax.ppermute(far_half.astype(BF), "tp", half_swap)
        joined = near + got_half.astype(F32)
        got_pair = lax.ppermute(joined[picked:].astype(BF), "tp", pair_swap)
        return (joined[:picked] + got_pair.astype(F32)).astype(BF)

    def across(rows):
        return lax.all_to_all(
            rows.reshape(peers, block, width), "tok", split_axis=0, concat_axis=0, tiled=True
        ).reshape(picked, width)

    returned = across(share_sum(mul(heads_rows, out_weight) + bias_full))
    own_in = mul(own_hot, tokens)
    own_cot_low = mul(own_hot, cotangent).astype(BF)
    own_cot = own_cot_low.astype(F32)
    gate = jax.nn.sigmoid(jnp.dot(own_in, router, precision=EXACT))
    branch = jnp.pad(returned.astype(F32), ((0, idle), (0, 0)))
    scale = jnp.where(jnp.arange(own) < picked, gate, 0.0)
    residual = own_in + scale[:, None] * branch
    second_hat, second_inv = normal_parts(residual)
    second = (second_hat * second_norm[0] + second_norm[1]).astype(BF)
    up_cols = up_all.transpose(1, 0, 2).reshape(width, -1)
    down_rows = down_all.reshape(-1, width)
    up_bias_all = lax.all_gather(up_bias, "tp", tiled=True)
    down_bias_all = lax.all_gather(down_bias, "tp", tiled=True)
    pre = mul(second, up_cols) + up_bias_all
    below = 0.5 * (1.0 + lax.erf(pre * 2.0 ** (-0.5)))
    bell = jnp.exp(-0.5 * pre * pre) * (2.0 * jnp.pi) ** (-0.5)
    hidden = (pre * below).astype(BF)
    layer_rows = (residual + mul(hidden, down_rows) + down_bias_all).astype(BF)
    d_hidden = mul_t1(own_cot_low, down_rows)
    d_pre = (d_hidden * (below + pre * bell)).astype(BF)
    d_down = mul_t0(hidden, own_cot_low).astype(BF).reshape(shares, -1, width)
    d_up = mul_t0(second, d_pre).astype(BF)
    d_up = d_up.reshape(width, shares, -1).transpose(1, 0, 2)
    d_second = mul_t1(d_pre, up_cols)
    d_residual = own_cot + norm_back(d_second, second_hat, second_inv, second_norm[0])
    d_branch = (d_residual[:picked] * scale[:picked, None]).astype(BF)
    d_logit = jnp.sum(d_residual * branch, axis=1) * scale * (1.0 - gate)
    small = jnp.concatenate(
        [
            jnp.sum(d_pre.astype(F32), axis=0).reshape(shares, width),
            jnp.stack(
                [
                    jnp.sum(d_second * second_hat, axis=0),
                    jnp.sum(d_second, axis=0),
                    jnp.sum(own_cot, axis=0),
                    jnp.sum(d_branch.astype(F32), axis=0),
                    jnp.sum(d_logit[:, None] * own_in, axis=0),
                ]
            ),
        ]
    )
    d_up_share = lax.psum_scatter(d_up, "tp", scatter_dimension=0)
    d_down_share = lax.psum_scatter(d_down, "tp", scatter_dimension=0)
    d_up_total = lax.psum(d_up_share, "tok").astype(F32)
    d_down_total = lax.psum(d_down_share, "tok").astype(F32)
    grad_own = across(d_branch)
    grad_near = jnp.concatenate([grad_own, lax.ppermute(grad_own, "tp", pair_swap)])
    grad_rows = jnp.concatenate([grad_near, lax.ppermute(grad_near, "tp", half_swap)])
    d_out_weight = mul_t0(heads_rows, grad_rows)
    d_heads_rows = mul_t1(grad_rows, out_weight).astype(BF)
    d_heads = mul(slot_hot, d_heads_rows).astype(BF).reshape(ROWS_DEV, pad, heads_local, HD)
    d_weights = jnp.einsum("rqhe,rkhe->rhqk", d_heads, value, preferred_element_type=F32)
    d_value = jnp.einsum("rhqk,rqhe->rkhe", weights_low, d_heads, preferred_element_type=F32)
    d_scores = (
        weights * (d_weights - jnp.sum(weights * d_weights, axis=-1, keepdims=True))
    ).astype(BF)
    d_query = jnp.einsum("rhqk,rkhe->rqhe", d_scores, key, preferred_element_type=F32) * score_scale
    d_key = jnp.einsum("rhqk,rqhe->rkhe", d_scores, query, preferred_element_type=F32) * score_scale
    d_qkv = (
        jnp.stack([d_query, d_key, d_value], axis=2).astype(BF).reshape(ROWS_DEV * pad, 3 * inner)
    )
    d_qkv_weight = mul_t0(slot_features, d_qkv)
    d_qkv_bias = jnp.sum(d_qkv.astype(F32), axis=0).reshape(3, inner)
    d_qv_bias = jnp.stack([d_qkv_bias[0], d_qkv_bias[2]])
    d_qkv_rows = mul_t0(slot_hot, d_qkv).astype(BF)
    d_normed = across(share_sum(mul_t1(d_qkv_rows, flat_weight))).astype(F32)
    d_qkv_total = lax.psum(d_qkv_weight.astype(BF), "tok").astype(F32)
    d_out_total = lax.psum(d_out_weight.astype(BF), "tok").astype(F32)
    first_hat, first_inv = normal_parts(own_in[:picked])
    d_picked = (
        d_residual[:picked]
        + norm_back(d_normed, first_hat, first_inv, first_norm[0])
        + d_logit[:picked, None] * router[None, :]
    ).astype(BF)
    d_idle = d_residual[picked:].astype(BF)

    def to_columns(rows):
        pieces = rows.reshape(rows.shape[0], shares, width // shares).transpose(1, 0, 2)
        return lax.all_to_all(pieces, "tp", split_axis=0, concat_axis=0, tiled=True).reshape(
            shares * rows.shape[0], width // shares
        )

    picked_hot = hot(back_picked, jnp.arange(shares * picked, dtype=jnp.int32))
    idle_hot = hot(back_idle, jnp.arange(shares * idle, dtype=jnp.int32))
    layer_out = (
        mul(picked_hot, to_columns(layer_rows[:picked]))
        + mul(idle_hot, to_columns(layer_rows[picked:]))
    ).astype(BF)
    d_tokens = mul(picked_hot, to_columns(d_picked)) + mul(idle_hot, to_columns(d_idle))
    first_pair = jnp.stack([jnp.sum(d_normed * first_hat, axis=0), jnp.sum(d_normed, axis=0)])
    small = lax.psum(jnp.concatenate([small, first_pair]), ("tok", "tp"))
    small_cols = columns_of(small[shares:], part, shares)
    d_up_bias = lax.dynamic_slice_in_dim(small, part, 1, 0).reshape(width)
    d_qv_bias = lax.psum(d_qv_bias, "tok")
    return (
        layer_out,
        d_tokens,
        d_qkv_total.reshape(width, 3, inner),
        d_qv_bias,
        d_out_total,
        small_cols[3],
        d_up_total,
        d_up_bias,
        d_down_total,
        small_cols[2],
        small_cols[5:7],
        small_cols[0:2],
        small_cols[4],
    )


def solution(mesh):
    return jax.shard_map(
        body,
        mesh=mesh,
        in_specs=(
            P("tok", None),
            P("tok"),
            P("tok"),
            P(),
            P(),
            P(None, None, "tp"),
            P(None, "tp"),
            P("tp", None),
            P("tp"),
            P(),
            P(None, "tp"),
            P("tp"),
            P("tp", None),
            P("tp"),
            P("tok", None),
        ),
        out_specs=(
            P("tok", "tp"),
            P("tok", "tp"),
            P(None, None, "tp"),
            P(None, "tp"),
            P("tp", None),
            P("tp"),
            P(None, "tp"),
            P("tp"),
            P("tp", None),
            P("tp"),
            P(None, "tp"),
            P(None, "tp"),
            P("tp"),
        ),
        check_vma=False,
    )
```

profile of v0, /device:TPU:0, one launch (start us, length us, event | category | flops | bytes accessed | tf_op | source)
XLA Modules:
  0.0 696.7 jit_solution(4545855774942127467)
XLA Ops:
  16.0 14.7 %fusion.135 = (f32[1152]{0:T(1024)S(1)}, f32[1152,768]{1,0:T(8,128)S(1)}) fusion(bf16[4616,768]{1,0:T(8,128)(2,1)} %param.15, s32[4616]{0:T(1024)S(1)} %get-tuple-element.46), kind=kOutput, calls=%fused_computation.269 | convolution fusion | flops 8174084096 | bytes 10652192 | tf_op jit(solution)/shard_map/dot_general | solution.py:37
  32.1 48.4 %all_to_all.40 = bf16[8,2,72,768]{3,2,1,0:T(8,128)(2,1)S(1)} all-to-all(bf16[8,2,72,768]{3,2,1,0:T(8,128)(2,1)S(1)} %broadcast_select_fusion), channel_id=1, replica_groups=mesh['tok'=8,'tp'=4] {'tok'}, dimensions={0} | all-to-all | bytes 3538944 | tf_op jit(solution)/shard_map/all_to_all | solution.py:130
  81.6 2.9 collective-permute-done
  85.6 3.9 pad_maximum_fusion
  89.7 12.9 %fusion.44 = bf16[2432,768]{1,0:T(8,128)(2,1)} fusion(bf16[2304,768]{1,0:T(8,128)(2,1)} %bitcast.217, s32[2304]{0:T(1024)S(1)} %eq.201, s32[2432]{0:T(1024)S(1)} %fusion.120), kind=kOutput, calls=%fused_computation.64 | convolution fusion | flops 8614182912 | bytes 7293440 | tf_op jit(solution)/shard_map/dot_general | solution.py:37
  102.6 3.8 select_reduce_fusion
  106.5 6.2 add_convert_fusion
  112.7 7.5 %reshape.344 = bf16[8,304,3,3,64]{1,0,4,3,2:T(8,128)(2,1)} reshape(bf16[2432,576]{0,1:T(8,128)(2,1)} %add_convert_fusion) | data formatting | bytes 5603328 | tf_op jit(solution)/shard_map/reshape | solution.py:155
  122.3 3.4 fusion.131
  125.7 8.3 %fusion.136 = (f32[8,3,304]{2,1,0:T(4,128)S(1)}, f32[8,3,304,304]{2,3,1,0:T(8,128)}) fusion(pred[8,304,304]{1,2,0:T(8,128)(4,1)} %compare_and_fusion, bf16[8,304,1,3,64]{1,0,4,3,2:T(8,128)(2,1)S(1)} %get-tuple-element.38, bf16[8,304,1,3,64]{1,0,4,3,2:T(8,128)(2,1)S(1)} %get-tuple-element.37), kind=kOutput, calls=%fused_computation.270 | convolution fusion | flops 292774176 | bytes 11508224 | tf_op jit(solution)/shard_map/sub | solution.py:161
  134.0 5.8 fusion.83
  141.4 4.1 fusion.53
  146.7 2.9 copy-done.4
  150.0 3.7 collective-permute-done.1
  153.7 3.3 slice_add_fusion.1
  158.5 15.1 %fusion.16 = f32[1200,768]{1,0:T(8,128)S(1)} fusion(bf16[4616,768]{1,0:T(8,128)(2,1)} %param.15, s32[4616]{0:T(1024)S(1)} %get-tuple-element.47), kind=kOutput, calls=%fused_computation.20 | convolution fusion | flops 8513750528 | bytes 10795040 | tf_op jit(solution)/shard_map/dot_general | solution.py:37
  175.6 3.2 convolution_reduce_fusion
  178.8 20.2 %all-gather.2 = f32[4,1,768]{2,1,0:T(1,128)S(1)} all-gather(f32[1,1,768]{2,1,0:T(1,128)S(1)} %reshape.375), channel_id=1, replica_groups=mesh['tok'=8,'tp'=4] {'tp'}, dimensions={0}, use_global_device_ids=true | all-gather | bytes 15360 | tf_op jit(solution)/shard_map/all_gather | solution.py:195
  200.2 3.6 all-to-all-start.1
  203.8 14.8 %fusion.65 = bf16[1200,768]{1,0:T(8,128)(2,1)} fusion(bf16[4616,768]{1,0:T(8,128)(2,1)} %param.29, s32[4616]{0:T(1024)S(1)} %get-tuple-element.47), kind=kOutput, calls=%fused_computation.100 | convolution fusion | flops 8514672128 | bytes 8951840 | tf_op jit(solution)/shard_map/dot_general | solution.py:37
  218.6 6.6 copy.121
  226.7 2.8 fusion.130
  231.2 10.5 %multiply_convert_fusion = (bf16[1200,3072]{1,0:T(8,128)(2,1)S(1)}, f32[1200,3072]{1,0:T(8,128)}) fusion(f32[3072]{0:T(1024)S(1)} %bitcast.228, bf16[768,3072]{0,1:T(8,128)(2,1)S(1)} %bitcast.209, f32[768]{0:T(1024)S(1)} %get-tuple-element.24, f32[768]{0:T(1024)S(1)} %get-tuple-element.23, f32[1200]{0:T(1024)S(1)} %add_rsqrt_fusion, ...), kind=kOutput, calls=%fused_computation.34 | convolution fusion | flops 5691801600 | bytes 31440960 | tf_op jit(solution)/shard_map/dot_general | solution.py:37
  241.7 8.3 %convolution_convert_fusion = bf16[3072,768]{1,0:T(8,128)(2,1)} fusion(bf16[1200,3072]{1,0:T(8,128)(2,1)S(1)} %get-tuple-element.67, bf16[1200,768]{1,0:T(8,128)(2,1)S(1)} %copy-done.16), kind=kOutput, calls=%fused_computation.65 | convolution fusion | flops 5664669696 | bytes 13934592 | tf_op jit(solution)/shard_map/dot_general | solution.py:41
  250.2 14.4 %convert_reduce_fusion = (f32[3072]{0:T(1024)}, bf16[1200,3072]{1,0:T(8,128)(2,1)S(1)}) fusion(f32[1200,3072]{1,0:T(8,128)} %get-tuple-element.68, bf16[1200,768]{1,0:T(8,128)(2,1)} %fusion.65, bf16[3072,768]{1,0:T(8,128)(2,1)} %all-gather.8.cloned.1.call-done), kind=kOutput, calls=%fused_computation.33 | convolution fusion | flops 5706544128 | bytes 28692480 | tf_op jit(solution)/shard_map/dot_general | solution.py:45
  264.6 13.4 %multiply_reduce_fusion.2 = (f32[768]{0:T(1024)}, f32[1200]{0:T(1024)S(1)}, f32[1200]{0:T(1024)S(1)}, f32[768]{0:T(1024)}, f32[1200,768]{1,0:T(8,128)S(1)}) fusion(f32[1200]{0:T(1024)S(1)} %add_rsqrt_fusion, f32[1200]{0:T(1024)S(1)} %broadcast_multiply_fusion.2, f32[1200,768]{1,0:T(8,128)S(1)} %copy-done.3, bf16[576,768]{1,0:T(8,128)(2,1)S(1)} %bitcast.199, ...), kind=kOutput, calls=%fused_computation.86 | convolution fusion | flops 5673365504 | bytes 20382144 | tf_op jit(solution)/shard_map/dot_general | solution.py:45
  278.0 4.2 fusion.60
  284.8 27.2 %all_to_all.41 = bf16[8,72,768]{2,1,0:T(8,128)(2,1)S(1)} all-to-all(bf16[8,72,768]{2,1,0:T(8,128)(2,1)S(1)} %bitcast.218), channel_id=1, replica_groups=mesh['tok'=8,'tp'=4] {'tok'}, dimensions={0} | all-to-all | bytes 1769472 | tf_op jit(solution)/shard_map/all_to_all | solution.py:179
  317.4 17.7 %all-reduce.4 = f32[768]{0:T(1024)} all-reduce(f32[768]{0:T(1024)} %dynamic-update-slice), channel_id=1, replica_groups=mesh['tok'=8,'tp'=4] {'tp'}, use_global_device_ids=true, to_apply=%add.4 | all-reduce | flops 768 | bytes 6144
  336.6 10.9 %convolution_convert_fusion.1 = bf16[768,3072]{1,0:T(8,128)(2,1)S(1)} fusion(bf16[1200,3072]{1,0:T(8,128)(2,1)} %copy-done.52, f32[768]{0:T(1024)} %copy-done.45, f32[768]{0:T(1024)} %copy-done.34, f32[1200]{0:T(1024)} %copy-done.31, f32[1200]{0:T(1024)S(1)} %broadcast_multiply_fusion.2, f32[1200,768]{1,0:T(8,128)} %copy-done.1, ...), kind=kOutput, calls=%fused_computation.66 | convolution fusion | flops 5672042496 | bytes 16683072 | tf_op jit(solution)/shard_map/dot_general | solution.py:41
  347.5 2.5 copy.186
  350.0 7.7 %fusion.56 = bf16[2432,192]{0,1:T(8,128)(2,1)} fusion(s32[2304]{0:T(1024)} %copy-done.39, s32[2432]{0:T(1024)} %copy-done.41, bf16[192,768]{1,0:T(8,128)(2,1)} %param.22, bf16[1152,768]{1,0:T(8,128)(2,1)} %collective-permute-done.4, bf16[576,768]{1,0:T(8,128)(2,1)S(1)} %collective-permute-done.3, bf16[576,768]{1,0:T(8,128)(2,1)S(1)} %bitcast.214), kind=kOutput, calls=%fused_computation.81 | convolution fusion | flops 2848284672 | bytes 4786688 | tf_op jit(solution)/shard_map/dot_general | solution.py:37
  357.8 2.6 reshape.354
  360.5 6.4 fusion.75
  366.8 8.9 %multiply_reduce_fusion = (f32[8,3,304]{2,1,0:T(4,128)S(1)}, f32[8,3,304,304]{2,3,1,0:T(8,128)}) fusion(f32[8,3,304,304]{2,3,1,0:T(8,128)} %get-tuple-element.66, f32[8,3,304]{2,1,0:T(4,128)S(1)} %copy-done.29, bf16[8,304,1,3,64]{1,0,4,3,2:T(8,128)(2,1)S(1)} %copy-done.18, bf16[8,304,3,64]{1,0,3,2:T(8,128)(2,1)S(1)} %reshape.354), kind=kOutput, calls=%fused_computation.40 | convolution fusion | flops 290548608 | bytes 19670016 | tf_op jit(solution)/shard_map/rqhe,rkhe->rhqk/dot_general | solution.py:235
  375.8 6.1 multiply_convert_fusion.1
  386.1 4.1 copy.131
  390.2 6.7 convert_element_type.200
  396.9 16.6 %fusion.62 = f32[2304,768]{1,0:T(8,128)} fusion(bf16[768,576]{0,1:T(8,128)(2,1)S(1)} %bitcast.192, bf16[2432,576]{0,1:T(8,128)(2,1)} %convert_element_type.200, s32[2304]{0:T(1024)S(1)} %copy-done.40, s32[2432]{0:T(1024)S(1)} %copy-done.42), kind=kOutput, calls=%fused_computation.98 | convolution fusion | flops 8500396032 | bytes 10783232 | tf_op jit(solution)/shard_map/dot_general | solution.py:45
  413.6 3.8 slice.288
  417.8 10.6 %fusion.64 = bf16[1200,768]{1,0:T(8,128)(2,1)S(1)} fusion(bf16[1200,3072]{1,0:T(8,128)(2,1)} %copy-done.54, bf16[3072,768]{1,0:T(8,128)(2,1)} %all-gather.8.cloned.1.call-done, f32[768]{0:T(1024)S(1)} %copy-done.49, f32[1200,768]{1,0:T(8,128)} %copy-done.1, bf16[576,768]{1,0:T(8,128)(2,1)S(1)} %bitcast.202, f32[1200]{0:T(1024)S(1)} %fusion.123), kind=kOutput, calls=%fused_computation.99 | convolution fusion | flops 5667840000 | bytes 18513600 | tf_op jit(solution)/shard_map/dot_general | solution.py:37
  431.0 3.5 all-to-all-start.2
  437.6 10.7 %all-to-all-done.2 = bf16[4,576,192]{1,2,0:T(8,128)(2,1)S(1)} async-done(((bf16[4,576,192]{1,2,0:T(8,128)(2,1)}), bf16[4,576,192]{1,2,0:T(8,128)(2,1)S(1)}, u32[]{:S(2)}, u32[]{:S(2)}) %all-to-all-start.2) | async-done | bytes 884768 | tf_op jit(solution)/shard_map/all_to_all | solution.py:262
  448.2 4.2 all-to-all-start.3
  462.2 4.1 all-to-all-done.3
  466.3 3.5 all-to-all-start.7
  469.8 2.9 copy.125
  472.7 2.7 reshape.351
  475.4 2.9 slice_add_fusion
  483.0 13.4 %fusion.2 = f32[4616,192]{0,1:T(8,128)} fusion(bf16[2496,192]{0,1:T(8,128)(2,1)} %reshape.351, s32[4616]{0:T(1024)S(1)} %copy-done.33), kind=kOutput, calls=%fused_computation.3 | convolution fusion | flops 4435791360 | bytes 4522016 | tf_op jit(solution)/shard_map/dot_general | solution.py:37
  496.5 6.8 collective-permute-done.6
  503.3 2.6 fusion.71
  505.9 4.7 all-to-all-start.5
  510.6 13.9 %fusion.40 = bf16[4616,192]{0,1:T(8,128)(2,1)} fusion(f32[4616,192]{0,1:T(8,128)} %fusion.2, bf16[2304,192]{0,1:T(8,128)(2,1)} %reshape.349, s32[4616]{0:T(1024)S(1)} %copy-done.32), kind=kOutput, calls=%fused_computation.57 | convolution fusion | flops 4096349184 | bytes 6220832 | tf_op jit(solution)/shard_map/dot_general | solution.py:37
  526.2 2.7 reshape.359
  529.0 4.0 fusion.86
  533.2 3.4 convolution_convert_fusion.3
  543.3 3.7 all-to-all-start.6
  547.0 13.5 %fusion.1 = f32[4616,192]{0,1:T(8,128)} fusion(bf16[2496,192]{0,1:T(8,128)(2,1)} %reshape.359, s32[4616]{0:T(1024)S(1)} %copy-done.33), kind=kOutput, calls=%fused_computation.2 | convolution fusion | flops 4435791360 | bytes 4522016 | tf_op jit(solution)/shard_map/dot_general | solution.py:37
  560.7 23.7 %psum.43 = f32[2,192]{1,0:T(2,128)} all-reduce(f32[2,192]{1,0:T(2,128)S(1)} %pad_maximum_fusion.8), channel_id=1, replica_groups=mesh['tok'=8,'tp'=4] {'tok'}, use_global_device_ids=true, to_apply=%region_22.23 | all-reduce | flops 384 | bytes 3072 | tf_op jit(solution)/shard_map/psum | solution.py:277
  584.4 38.3 %psum.45 = f32[11,768]{1,0:T(8,128)S(1)} all-reduce(f32[11,768]{1,0:T(8,128)S(1)} %concatenate.16), channel_id=1, replica_groups=mesh['tok'=8,'tp'=4] {'tok','tp'}, use_global_device_ids=true, to_apply=%region_32.33 | all-reduce | flops 8448 | bytes 67584 | tf_op jit(solution)/shard_map/psum | solution.py:274
  626.1 13.6 %fusion.39 = f32[4616,192]{0,1:T(8,128)} fusion(f32[4616,192]{0,1:T(8,128)} %fusion.1, bf16[2304,192]{0,1:T(8,128)(2,1)S(1)} %reshape.357, s32[4616]{0:T(1024)S(1)} %copy-done.32), kind=kOutput, calls=%fused_computation.56 | convolution fusion | flops 4095462912 | bytes 7993376 | tf_op jit(solution)/shard_map/dot_general | solution.py:37
  639.7 42.5 %all-reduce.8.cloned.1.call-done = (bf16[768,3,192]{0,2,1:T(8,128)(2,1)}, bf16[192,768]{1,0:T(8,128)(2,1)}, bf16[768,768]{1,0:T(8,128)(2,1)}, bf16[768,768]{1,0:T(8,128)(2,1)}) async-done(((bf16[768,3,192]{0,2,1:T(8,128)(2,1)}, bf16[192,768]{1,0:T(8,128)(2,1)}, bf16[768,768]{1,0:T(8,128)(2,1)}, bf16[768,768]{1,0:T(8,128)(2,1)}), (bf16[768,3,192]{0,2,1:T(8,128)(2,1)}, bf16[192,768]{1,0:T(8,128)(2,1)}, ...) | async-done | bytes 3538960 | tf_op jit(solution)/shard_map/psum | solution.py:250
  684.2 2.5 reshape.361
  (269 shorter events, 76.2 us)
Async XLA Ops:
  7.2 99.3 %copy-start = (bf16[768,3,192]{0,2,1:T(8,128)(2,1)S(1)}, bf16[768,3,192]{0,2,1:T(8,128)(2,1)}, u32[]{:S(2)}) copy-start(bf16[768,3,192]{0,2,1:T(8,128)(2,1)} %param.20) | copy-start | bytes 2654212
  7.2 211.4 %all-gather.6.cloned.1.call-start = ((), (), s32[]{:S(2)}) async-start(), calls=%async_computation.12 | async-start | bytes 5898240 | tf_op jit(solution)/shard_map/all_gather | solution.py:112
  8.1 23.2 %copy-start.23 = (f32[768]{0:T(1024)}, f32[768]{0:T(1024)S(1)}, u32[]{:S(2)}) copy-start(f32[768]{0:T(1024)S(1)} %get-tuple-element.21) | copy-start | bytes 9220
  32.1 49.1 %copy-start.51 = (f32[192]{0:T(256)S(1)}, f32[192]{0:T(256)}, u32[]{:S(2)}) copy-start(f32[192]{0:T(256)} %param.23) | copy-start | bytes 2308
  32.1 49.4 %copy-start.50 = (f32[2,192]{1,0:T(2,128)S(1)}, f32[2,192]{1,0:T(2,128)}, u32[]{:S(2)}) copy-start(f32[2,192]{1,0:T(2,128)} %param.21) | copy-start | bytes 4612
  80.6 3.9 collective-permute-start
  80.7 169.5 %all-gather.8.cloned.1.call-start = ((), (), s32[]{:S(2)}) async-start(), calls=%async_computation.13 | async-start | bytes 5898240 | tf_op jit(solution)/shard_map/all_gather | solution.py:113
  81.6 59.8 %copy-start.41 = (s32[2432]{0:T(1024)}, s32[2432]{0:T(1024)S(1)}, u32[]{:S(2)}) copy-start(s32[2432]{0:T(1024)S(1)} %fusion.120) | copy-start | bytes 29188
  89.7 51.7 %copy-start.39 = (s32[2304]{0:T(1024)}, s32[2304]{0:T(1024)S(1)}, u32[]{:S(2)}) copy-start(s32[2304]{0:T(1024)S(1)} %eq.201) | copy-start | bytes 27652
  125.7 8.3 %copy-start.7 = (bf16[8,304,1,3,64]{1,0,4,3,2:T(8,128)(2,1)}, bf16[8,304,1,3,64]{1,0,4,3,2:T(8,128)(2,1)S(1)}, u32[]{:S(2)}) copy-start(bf16[8,304,1,3,64]{1,0,4,3,2:T(8,128)(2,1)S(1)} %get-tuple-element.37) | copy-start | bytes 2801668
  125.7 8.3 %copy-start.10 = (bf16[8,304,1,3,64]{1,0,4,3,2:T(8,128)(2,1)}, bf16[8,304,1,3,64]{1,0,4,3,2:T(8,128)(2,1)S(1)}, u32[]{:S(2)}) copy-start(bf16[8,304,1,3,64]{1,0,4,3,2:T(8,128)(2,1)S(1)} %get-tuple-element.38) | copy-start | bytes 2801668
  134.0 5.8 copy-start.28
  149.8 3.9 collective-permute-start.1
  157.1 42.0 %collective-permute-start.2 = (bf16[576,768]{1,0:T(8,128)(2,1)S(1)}, bf16[576,768]{1,0:T(8,128)(2,1)S(1)}, u32[]{:S(2)}, u32[]{:S(2)}) collective-permute-start(bf16[576,768]{1,0:T(8,128)(2,1)S(1)} %slice.292), channel_id=1, source_target_pairs={{0,2},{1,3},{2,0},{3,1},{4,6},{5,7},{6,4},{7,5},{8,10},{9,11},{10,... | collective-permute-start | bytes 2654216 | tf_op jit(solution)/shard_map/ppermute | solution.py:175
  158.5 15.1 %copy-start.46 = (f32[768]{0:T(1024)S(1)}, f32[768]{0:T(1024)}, u32[]{:S(2)}) copy-start(f32[768]{0:T(1024)} %param.26) | copy-start | bytes 9220
  158.5 15.2 %copy-start.35 = (f32[768]{0:T(1024)S(1)}, f32[768]{0:T(1024)}, u32[]{:S(2)}) copy-start(f32[768]{0:T(1024)} %param.18) | copy-start | bytes 9220
  173.6 25.4 %copy-start.44 = (f32[2,768]{1,0:T(2,128)S(1)}, f32[2,768]{1,0:T(2,128)}, u32[]{:S(2)}) copy-start(f32[2,768]{1,0:T(2,128)} %param.24) | copy-start | bytes 18436
  178.8 21.4 %copy-start.25 = (f32[1200]{0:T(1024)}, f32[1200]{0:T(1024)S(1)}, u32[]{:S(2)}) copy-start(f32[1200]{0:T(1024)S(1)} %convolution_reduce_fusion) | copy-start | bytes 14404
  199.0 31.7 %copy-start.45 = (f32[768]{0:T(1024)}, f32[768]{0:T(1024)S(1)}, u32[]{:S(2)}) copy-start(f32[768]{0:T(1024)S(1)} %get-tuple-element.24) | copy-start | bytes 9220
  199.1 78.9 %copy-start.34 = (f32[768]{0:T(1024)}, f32[768]{0:T(1024)S(1)}, u32[]{:S(2)}) copy-start(f32[768]{0:T(1024)S(1)} %get-tuple-element.23) | copy-start | bytes 9220
  200.2 26.5 %all-to-all-start.1 = ((bf16[8,72,768]{2,1,0:T(8,128)(2,1)}), bf16[8,72,768]{2,1,0:T(8,128)(2,1)S(1)}, u32[]{:S(2)}, u32[]{:S(2)}) async-start(bf16[8,72,768]{2,1,0:T(8,128)(2,1)} %bitcast.21), calls=%async_computation.1 | async-start | bytes 1769472 | tf_op jit(solution)/shard_map/all_to_all | solution.py:179
  203.7 335.6 %reduce-scatter.5.cloned.1.call-start = ((), (), s32[]{:S(2)}) async-start(), calls=%async_computation.11 | async-start | bytes 5898240 | tf_op jit(solution)/shard_map/reduce_scatter | solution.py:226
  226.7 4.6 copy-start.9
  230.8 47.2 %copy-start.31 = (f32[1200]{0:T(1024)}, f32[1200]{0:T(1024)S(1)}, u32[]{:S(2)}) copy-start(f32[1200]{0:T(1024)S(1)} %add_rsqrt_fusion) | copy-start | bytes 14404
  231.2 10.5 %copy-start.16 = (bf16[1200,768]{1,0:T(8,128)(2,1)S(1)}, bf16[1200,768]{1,0:T(8,128)(2,1)}, u32[]{:S(2)}) copy-start(bf16[1200,768]{1,0:T(8,128)(2,1)} %fusion.65) | copy-start | bytes 5529604
  241.7 8.3 %copy-start.54 = (bf16[1200,3072]{1,0:T(8,128)(2,1)}, bf16[1200,3072]{1,0:T(8,128)(2,1)S(1)}, u32[]{:S(2)}) copy-start(bf16[1200,3072]{1,0:T(8,128)(2,1)S(1)} %get-tuple-element.67) | copy-start | bytes 22118404
  250.1 289.3 %reduce-scatter.3.cloned.1.call-start = ((), (), s32[]{:S(2)}) async-start(), calls=%async_computation.10 | async-start | bytes 5898240 | tf_op jit(solution)/shard_map/reduce_scatter | solution.py:225
  250.2 14.4 %copy-start.3 = (f32[1200,768]{1,0:T(8,128)S(1)}, f32[1200,768]{1,0:T(8,128)}, u32[]{:S(2)}) copy-start(f32[1200,768]{1,0:T(8,128)} %copy-done.1) | copy-start | bytes 11059204
  264.5 13.4 %copy-start.52 = (bf16[1200,3072]{1,0:T(8,128)(2,1)}, bf16[1200,3072]{1,0:T(8,128)(2,1)S(1)}, u32[]{:S(2)}) copy-start(bf16[1200,3072]{1,0:T(8,128)(2,1)S(1)} %get-tuple-element.73) | copy-start | bytes 22118404
  264.6 13.5 %copy-start.17 = (bf16[1200,768]{1,0:T(8,128)(2,1)S(1)}, bf16[1200,768]{1,0:T(8,128)(2,1)}, u32[]{:S(2)}) copy-start(bf16[1200,768]{1,0:T(8,128)(2,1)} %fusion.65) | copy-start | bytes 5529604
  312.0 38.1 %copy-start.13 = (bf16[8,72,768]{2,1,0:T(8,128)(2,1)}, bf16[8,72,768]{2,1,0:T(8,128)(2,1)S(1)}, u32[]{:S(2)}) copy-start(bf16[8,72,768]{2,1,0:T(8,128)(2,1)S(1)} %all_to_all.41) | copy-start | bytes 2654212
  312.0 23.2 %collective-permute-start.3 = (bf16[576,768]{1,0:T(8,128)(2,1)S(1)}, bf16[576,768]{1,0:T(8,128)(2,1)S(1)}, u32[]{:S(2)}, u32[]{:S(2)}) collective-permute-start(bf16[576,768]{1,0:T(8,128)(2,1)S(1)} %bitcast.212), channel_id=1, source_target_pairs={{0,2},{1,3},{2,0},{3,1},{4,6},{5,7},{6,4},{7,5},{8,10},{9,11},{10,... | collective-permute-start | bytes 2654216 | tf_op jit(solution)/shard_map/ppermute | solution.py:230
  335.2 14.9 %copy-start.21 = (bf16[576,768]{1,0:T(8,128)(2,1)}, bf16[576,768]{1,0:T(8,128)(2,1)S(1)}, u32[]{:S(2)}) copy-start(bf16[576,768]{1,0:T(8,128)(2,1)S(1)} %collective-permute-done.3) | copy-start | bytes 2654212
  336.6 13.4 %collective-permute-start.4 = (bf16[1152,768]{1,0:T(8,128)(2,1)}, bf16[1152,768]{1,0:T(8,128)(2,1)}, u32[]{:S(2)}, u32[]{:S(2)}) collective-permute-start(bf16[1152,768]{1,0:T(8,128)(2,1)} %pad_maximum_fusion.2), channel_id=1, source_target_pairs={{0,1},{1,0},{2,3},{3,2},{4,5},{5,4},{6,7},{7,6},{8,9},{9,8},{10,11... | collective-permute-start | bytes 5308424 | tf_op jit(solution)/shard_map/ppermute | solution.py:231
  360.4 6.4 copy-start.18
  360.4 6.4 copy-start.29
  360.4 15.3 %slice-start = ((s8[11206656]{0:T(1024)(128)(4,1)}), s8[4194304]{0:T(1024)(128)(4,1)S(1)}, s32[]{:S(2)}) async-start(s8[11206656]{0:T(1024)(128)(4,1)} %bitcast.203), calls=%async_computation.15 | async-start | bytes 8388608
  360.4 15.3 %slice-start.1 = ((s8[11206656]{0:T(1024)(128)(4,1)}), s8[4194304]{0:T(1024)(128)(4,1)S(1)}, s32[]{:S(2)}) async-start(s8[11206656]{0:T(1024)(128)(4,1)} %bitcast.203), calls=%async_computation.16 | async-start | bytes 8388608
  366.8 8.9 %slice-start.2 = ((s8[11206656]{0:T(1024)(128)(4,1)}), s8[2818048]{0:T(1024)(128)(4,1)S(1)}, s32[]{:S(2)}) async-start(s8[11206656]{0:T(1024)(128)(4,1)} %bitcast.203), calls=%async_computation.17 | async-start | bytes 5636096
  375.7 6.2 copy-start.11
  390.2 6.7 copy-start.40
  390.2 6.7 copy-start.42
  396.9 20.9 %copy-start.49 = (f32[768]{0:T(1024)S(1)}, f32[768]{0:T(1024)}, u32[]{:S(2)}) copy-start(f32[768]{0:T(1024)} %all-reduce.4) | copy-start | bytes 9220
  417.3 58.1 %collective-permute-start.5 = (bf16[1152,768]{1,0:T(8,128)(2,1)}, bf16[1152,768]{1,0:T(8,128)(2,1)}, u32[]{:S(2)}, u32[]{:S(2)}) collective-permute-start(bf16[1152,768]{1,0:T(8,128)(2,1)} %slice.288), channel_id=1, source_target_pairs={{0,1},{1,0},{2,3},{3,2},{4,5},{5,4},{6,7},{7,6},{8,9},{9,8},{10,11... | collective-permute-start | bytes 5308424 | tf_op jit(solution)/shard_map/ppermute | solution.py:173
  429.7 6.5 slice-start.3
  431.0 17.2 %all-to-all-start.2 = ((bf16[4,576,192]{1,2,0:T(8,128)(2,1)}), bf16[4,576,192]{1,2,0:T(8,128)(2,1)S(1)}, u32[]{:S(2)}, u32[]{:S(2)}) async-start(bf16[4,576,192]{1,2,0:T(8,128)(2,1)} %bitcast.29), calls=%async_computation.2 | async-start | bytes 1966080 | tf_op jit(solution)/shard_map/all_to_all | solution.py:262
  436.2 19.8 %copy-start.43 = (f32[3072]{0:T(1024)S(1)}, f32[3072]{0:T(1024)}, u32[]{:S(2)}) copy-start(f32[3072]{0:T(1024)} %get-tuple-element.72) | copy-start | bytes 36868
  436.2 19.8 %copy-start.48 = (f32[768]{0:T(1024)S(1)}, f32[768]{0:T(1024)}, u32[]{:S(2)}) copy-start(f32[768]{0:T(1024)} %get-tuple-element.13) | copy-start | bytes 9220
  436.2 19.8 %copy-start.47 = (f32[768]{0:T(1024)S(1)}, f32[768]{0:T(1024)}, u32[]{:S(2)}) copy-start(f32[768]{0:T(1024)} %get-tuple-element.18) | copy-start | bytes 9220
  436.2 19.8 %copy-start.38 = (f32[768]{0:T(1024)S(1)}, f32[768]{0:T(1024)}, u32[]{:S(2)}) copy-start(f32[768]{0:T(1024)} %get-tuple-element.40) | copy-start | bytes 9220
  436.2 19.8 %copy-start.26 = (f32[1200]{0:T(1024)S(1)}, f32[1200]{0:T(1024)}, u32[]{:S(2)}) copy-start(f32[1200]{0:T(1024)} %copy-done.25) | copy-start | bytes 14404
  436.2 19.8 %copy-start.30 = (f32[1200]{0:T(1024)S(1)}, f32[1200]{0:T(1024)}, u32[]{:S(2)}) copy-start(f32[1200]{0:T(1024)} %get-tuple-element.33) | copy-start | bytes 14404
  448.2 18.1 %all-to-all-start.3 = ((bf16[4,624,192]{1,2,0:T(8,128)(2,1)}), bf16[4,624,192]{1,2,0:T(8,128)(2,1)}, u32[]{:S(2)}, u32[]{:S(2)}) async-start(bf16[4,624,192]{1,2,0:T(8,128)(2,1)} %bitcast.31), calls=%async_computation.3 | async-start | bytes 1966080 | tf_op jit(solution)/shard_map/all_to_all | solution.py:262
  452.5 6.0 copy-start.37
  456.1 4.5 copy-start.27
  466.3 39.6 %all-to-all-start.7 = ((bf16[4,624,192]{1,2,0:T(8,128)(2,1)}), bf16[4,624,192]{1,2,0:T(8,128)(2,1)S(1)}, u32[]{:S(2)}, u32[]{:S(2)}) async-start(bf16[4,624,192]{1,2,0:T(8,128)(2,1)} %bitcast.211), calls=%async_computation.7 | async-start | bytes 1966080 | tf_op jit(solution)/shard_map/all_to_all | solution.py:262
  475.4 7.6 %copy-start.33 = (s32[4616]{0:T(1024)S(1)}, s32[4616]{0:T(1024)}, u32[]{:S(2)}) copy-start(s32[4616]{0:T(1024)} %get-tuple-element.49) | copy-start | bytes 55396
  481.1 22.2 %collective-permute-start.6 = (bf16[576,768]{1,0:T(8,128)(2,1)}, bf16[576,768]{1,0:T(8,128)(2,1)S(1)}, u32[]{:S(2)}, u32[]{:S(2)}) collective-permute-start(bf16[576,768]{1,0:T(8,128)(2,1)} %slice.291), channel_id=1, source_target_pairs={{0,2},{1,3},{2,0},{3,1},{4,6},{5,7},{6,4},{7,5},{8,10},{9,11},{10,... | collective-permute-start | bytes 2654216 | tf_op jit(solution)/shard_map/ppermute | solution.py:175
  496.5 14.1 %copy-start.32 = (s32[4616]{0:T(1024)S(1)}, s32[4616]{0:T(1024)}, u32[]{:S(2)}) copy-start(s32[4616]{0:T(1024)} %get-tuple-element.45) | copy-start | bytes 55396
  505.9 30.6 %all-to-all-start.5 = ((bf16[8,72,768]{2,1,0:T(8,128)(2,1)}), bf16[8,72,768]{2,1,0:T(8,128)(2,1)S(1)}, u32[]{:S(2)}, u32[]{:S(2)}) async-start(bf16[8,72,768]{2,1,0:T(8,128)(2,1)} %bitcast.216), calls=%async_computation.5 | async-start | bytes 1769472 | tf_op jit(solution)/shard_map/all_to_all | solution.py:179
  510.6 171.6 %all-reduce.8.cloned.1.call-start = ((), (), s32[]{:S(2)}) async-start(), calls=%async_computation.14 | async-start | bytes 7077888 | tf_op jit(solution)/shard_map/psum | solution.py:250
  543.3 81.4 %all-to-all-start.6 = ((bf16[4,576,192]{1,2,0:T(8,128)(2,1)}), bf16[4,576,192]{1,2,0:T(8,128)(2,1)S(1)}, u32[]{:S(2)}, u32[]{:S(2)}) async-start(bf16[4,576,192]{1,2,0:T(8,128)(2,1)} %bitcast.43), calls=%async_computation.6 | async-start | bytes 1966080 | tf_op jit(solution)/shard_map/all_to_all | solution.py:262
  682.2 4.5 copy-start.20
  682.2 6.1 copy-start.19
  (14 other events, 36.3 us)
Sparse Core Ops, SparseCore 0:
  80.8 36.5 all-gather.5
  150.1 55.4 all-gather.7
  250.2 47.7 reduce-scatter.4
  350.1 46.8 reduce-scatter.2
  539.5 142.6 all-reduce.7
where the time goes:
time: 705 us; the launch traced here: 697 us
  matrix products  260 us (37%)
  blocking collectives  175 us (25%)
  local copies, waits for them, and re-layouts  80 us (11%)
  waiting for transfers between devices  72.2 us (10%)
  other arithmetic  63.8 us (9%)
  starting transfers between devices  29.5 us (4%)
  between operations  16.1 us (2%)
    dot_general x14, matrix products, mul(): lax.dot_general(left, right, (((1,), (0,)), ((), ())), preferred_element_...  149 us
    all_to_all x1, blocking collectives, body(): lax.all_to_all(send_rows.reshape(peers, 2, block, width), 'tok', split_ax...  48.4 us
    dot_general x3, matrix products, mul_t1(): lax.dot_general(left, right, (((1,), (1,)), ((), ())), preferred_element_...  44.5 us
    psum x1, waiting for transfers between devices, body(): d_qkv_total = lax.psum(d_qkv_weight.astype(BF), 'tok').astype(F32)  42.5 us
    psum x1, blocking collectives, body(): small = lax.psum(jnp.concatenate([small, first_pair]), ('tok', 'tp'))  38.3 us
    dot_general x5, matrix products, mul_t0(): lax.dot_general(left, right, (((0,), (0,)), ((), ())), preferred_element_...  30.6 us
    all_to_all x1, blocking collectives, across(): lax.all_to_all(rows.reshape(peers, block, width), 'tok', split_axis=0, co...  27.2 us
    psum x1, blocking collectives, body(): d_qv_bias = lax.psum(d_qv_bias, 'tok')  23.7 us
  transfers between devices with their start and end apart: 18, of which 7 were waited for; matrix products, arithmetic and copies ran while one was open for 52% of the time, Pallas kernels for 0%

commit v1 on v0

--- a/solution.py
+++ b/solution.py
@@ -274,7 +274,16 @@
     small = lax.psum(jnp.concatenate([small, first_pair]), ("tok", "tp"))
     small_cols = columns_of(small[shares:], part, shares)
     d_up_bias = lax.dynamic_slice_in_dim(small, part, 1, 0).reshape(width)
-    d_qv_bias = lax.psum(d_qv_bias, "tok")
+
+    def begin_the_weights(local_x):
+        parts_n = lax.axis_size("tok")
+        found_now = local_x
+        plain = lambda out_arr: [(ix, ix ^ out_arr) for ix in range(parts_n)]
+        for p in range(parts_n.bit_length() - 1):
+            found_now = found_now + lax.ppermute(found_now, axis_name="tok", perm=plain(1 << p))
+        return found_now
+
+    d_qv_bias = begin_the_weights(d_qv_bias)
     return (
         layer_out,
         d_tokens,

time: 705 us -> 679 us (0.963)
  blocking collectives: 175 us -> 116 us
  waiting for transfers between devices: 72.2 us -> 92.6 us
  starting transfers between devices: 29.5 us -> 43.3 us
    all_to_all x1 -> x0, blocking collectives: 27.2 us -> none  [across(): lax.all_to_all(rows.reshape(peers, block, width), 'tok', split_axis=0, co...]
    psum x1 -> x0, blocking collectives: 23.7 us -> none  [body(): d_qv_bias = lax.psum(d_qv_bias, 'tok')]
    all_to_all x4, waiting for transfers between devices: 14.8 us -> 0.01 us  [to_columns(): lax.all_to_all(pieces, 'tp', split_axis=0, concat_axis=0, tiled=True)]
    psum x1, waiting for transfers between devices: 42.5 us -> 56.6 us  [body(): d_qkv_total = lax.psum(d_qkv_weight.astype(BF), 'tok').astype(F32)]
    all_to_all x2 -> x3, waiting for transfers between devices: 1.41 us -> 14.9 us  [across(): lax.all_to_all(rows.reshape(peers, block, width), 'tok', split_axis=0, co...]
    unnamed x1, blocking collectives: 17.7 us -> 6.65 us
    ppermute x0 -> x3, starting transfers between devices: none -> 8.18 us  [begin_the_weights(): lax.ppermute(found_now, axis_name='tok', perm=plain(1 << p))]
    ppermute x1, waiting for transfers between devices: 0.01 us -> 7.61 us  [body(): lax.ppermute(grad_own, 'tp', pair_swap)]
  transfers between devices with their start and end apart: 18 -> 22, of which waited for: 7 -> 9; matrix products, arithmetic and copies ran while one was open for 52% -> 54% of each run, Pallas kernels for 0% -> 0%
where the time goes in v1:
time: 679 us; the launch traced here: 670 us
  matrix products  261 us (38%)
  blocking collectives  116 us (17%)
  waiting for transfers between devices  92.6 us (14%)
  local copies, waits for them, and re-layouts  77.4 us (11%)
  other arithmetic  64.6 us (10%)
  starting transfers between devices  43.3 us (6%)
  between operations  16 us (2%)
    dot_general x14, matrix products, mul(): lax.dot_general(left, right, (((1,), (0,)), ((), ())), preferred_element_...  148 us
    psum x1, waiting for transfers between devices, body(): d_qkv_total = lax.psum(d_qkv_weight.astype(BF), 'tok').astype(F32)  56.6 us
    all_to_all x1, blocking collectives, body(): lax.all_to_all(send_rows.reshape(peers, 2, block, width), 'tok', split_ax...  48.4 us
    dot_general x3, matrix products, mul_t1(): lax.dot_general(left, right, (((1,), (1,)), ((), ())), preferred_element_...  44.3 us
    psum x1, blocking collectives, body(): small = lax.psum(jnp.concatenate([small, first_pair]), ('tok', 'tp'))  40.4 us
    dot_general x5, matrix products, mul_t0(): lax.dot_general(left, right, (((0,), (0,)), ((), ())), preferred_element_...  32 us
    all_gather x1, blocking collectives, body(): up_bias_all = lax.all_gather(up_bias, 'tp', tiled=True)  20.2 us
    all_to_all x4, starting transfers between devices, to_columns(): lax.all_to_all(pieces, 'tp', split_axis=0, concat_axis=0, tiled=True)  15.3 us
  transfers between devices with their start and end apart: 22, of which 9 were waited for; matrix products, arithmetic and copies ran while one was open for 54% of the time, Pallas kernels for 0%

profile of v1, /device:TPU:0, one launch (start us, length us, event | category | flops | bytes accessed | tf_op | source)
XLA Modules:
  0.0 670.3 jit_solution(3554169331562140585)
XLA Ops:
  16.0 14.7 %fusion.136 = (f32[1152]{0:T(1024)S(1)}, f32[1152,768]{1,0:T(8,128)S(1)}) fusion(bf16[4616,768]{1,0:T(8,128)(2,1)} %param.15, s32[4616]{0:T(1024)S(1)} %get-tuple-element.46), kind=kOutput, calls=%fused_computation.270 | convolution fusion | flops 8174084096 | bytes 10652192 | tf_op jit(solution)/shard_map/dot_general | solution.py:37
  32.1 48.4 %all_to_all.40 = bf16[8,2,72,768]{3,2,1,0:T(8,128)(2,1)S(1)} all-to-all(bf16[8,2,72,768]{3,2,1,0:T(8,128)(2,1)S(1)} %broadcast_select_fusion), channel_id=1, replica_groups=mesh['tok'=8,'tp'=4] {'tok'}, dimensions={0} | all-to-all | bytes 3538944 | tf_op jit(solution)/shard_map/all_to_all | solution.py:130
  81.6 2.9 collective-permute-done
  85.6 3.9 pad_maximum_fusion
  89.7 12.9 %fusion.44 = bf16[2432,768]{1,0:T(8,128)(2,1)} fusion(bf16[2304,768]{1,0:T(8,128)(2,1)} %bitcast.216, s32[2304]{0:T(1024)S(1)} %eq.201, s32[2432]{0:T(1024)S(1)} %fusion.120), kind=kOutput, calls=%fused_computation.64 | convolution fusion | flops 8614182912 | bytes 7293440 | tf_op jit(solution)/shard_map/dot_general | solution.py:37
  102.6 3.8 select_reduce_fusion
  106.5 6.1 add_convert_fusion
  112.6 7.5 %reshape.344 = bf16[8,304,3,3,64]{1,0,4,3,2:T(8,128)(2,1)} reshape(bf16[2432,576]{0,1:T(8,128)(2,1)} %add_convert_fusion) | data formatting | bytes 5603328 | tf_op jit(solution)/shard_map/reshape | solution.py:155
  122.2 3.4 fusion.132
  125.6 8.3 %fusion.137 = (f32[8,3,304]{2,1,0:T(4,128)S(1)}, f32[8,3,304,304]{2,3,1,0:T(8,128)}) fusion(pred[8,304,304]{1,2,0:T(8,128)(4,1)} %compare_and_fusion, bf16[8,304,1,3,64]{1,0,4,3,2:T(8,128)(2,1)S(1)} %get-tuple-element.38, bf16[8,304,1,3,64]{1,0,4,3,2:T(8,128)(2,1)S(1)} %get-tuple-element.37), kind=kOutput, calls=%fused_computation.271 | convolution fusion | flops 292774176 | bytes 11508224 | tf_op jit(solution)/shard_map/sub | solution.py:161
  134.0 5.8 fusion.83
  141.4 4.1 fusion.53
  146.7 2.9 copy-done.5
  149.9 3.7 collective-permute-done.1
  153.6 3.3 slice_add_fusion.1
  158.4 15.1 %fusion.16 = f32[1200,768]{1,0:T(8,128)S(1)} fusion(bf16[4616,768]{1,0:T(8,128)(2,1)} %param.15, s32[4616]{0:T(1024)S(1)} %copy-done.43), kind=kOutput, calls=%fused_computation.20 | convolution fusion | flops 8513750528 | bytes 10795040 | tf_op jit(solution)/shard_map/dot_general | solution.py:37
  175.4 3.2 convolution_reduce_fusion
  178.7 20.2 %all-gather.2 = f32[4,1,768]{2,1,0:T(1,128)S(1)} all-gather(f32[1,1,768]{2,1,0:T(1,128)S(1)} %reshape.375), channel_id=1, replica_groups=mesh['tok'=8,'tp'=4] {'tp'}, dimensions={0}, use_global_device_ids=true | all-gather | bytes 15360 | tf_op jit(solution)/shard_map/all_gather | solution.py:195
  200.0 3.6 all-to-all-start.1
  203.6 14.8 %fusion.65 = bf16[1200,768]{1,0:T(8,128)(2,1)} fusion(bf16[4616,768]{1,0:T(8,128)(2,1)} %param.29, s32[4616]{0:T(1024)S(1)} %copy-done.43), kind=kOutput, calls=%fused_computation.100 | convolution fusion | flops 8514672128 | bytes 8951840 | tf_op jit(solution)/shard_map/dot_general | solution.py:37
  218.5 6.6 copy.121
  226.5 2.8 fusion.131
  231.1 10.5 %multiply_convert_fusion = (bf16[1200,3072]{1,0:T(8,128)(2,1)S(1)}, f32[1200,3072]{1,0:T(8,128)}) fusion(f32[3072]{0:T(1024)S(1)} %bitcast.226, bf16[768,3072]{0,1:T(8,128)(2,1)S(1)} %bitcast.209, f32[768]{0:T(1024)S(1)} %get-tuple-element.24, f32[768]{0:T(1024)S(1)} %get-tuple-element.23, f32[1200]{0:T(1024)S(1)} %add_rsqrt_fusion, ...), kind=kOutput, calls=%fused_computation.34 | convolution fusion | flops 5691801600 | bytes 31440960 | tf_op jit(solution)/shard_map/dot_general | solution.py:37
  241.6 8.3 %convolution_convert_fusion = bf16[3072,768]{1,0:T(8,128)(2,1)} fusion(bf16[1200,3072]{1,0:T(8,128)(2,1)S(1)} %get-tuple-element.67, bf16[1200,768]{1,0:T(8,128)(2,1)S(1)} %copy-done.19), kind=kOutput, calls=%fused_computation.65 | convolution fusion | flops 5664669696 | bytes 13934592 | tf_op jit(solution)/shard_map/dot_general | solution.py:41
  250.0 14.4 %convert_reduce_fusion = (f32[3072]{0:T(1024)}, bf16[1200,3072]{1,0:T(8,128)(2,1)S(1)}) fusion(f32[1200,3072]{1,0:T(8,128)} %get-tuple-element.68, bf16[1200,768]{1,0:T(8,128)(2,1)} %fusion.65, bf16[3072,768]{1,0:T(8,128)(2,1)} %all-gather.8.cloned.1.call-done), kind=kOutput, calls=%fused_computation.33 | convolution fusion | flops 5706544128 | bytes 28692480 | tf_op jit(solution)/shard_map/dot_general | solution.py:45
  264.3 13.4 %multiply_reduce_fusion.2 = (f32[768]{0:T(1024)}, f32[1200]{0:T(1024)S(1)}, f32[1200]{0:T(1024)S(1)}, f32[768]{0:T(1024)}, f32[1200,768]{1,0:T(8,128)S(1)}) fusion(f32[1200]{0:T(1024)S(1)} %add_rsqrt_fusion, f32[1200]{0:T(1024)S(1)} %broadcast_multiply_fusion.2, f32[1200,768]{1,0:T(8,128)S(1)} %copy-done.3, bf16[576,768]{1,0:T(8,128)(2,1)S(1)} %bitcast.199, ...), kind=kOutput, calls=%fused_computation.86 | convolution fusion | flops 5673365504 | bytes 20382144 | tf_op jit(solution)/shard_map/dot_general | solution.py:45
  277.7 4.1 fusion.60
  285.4 4.7 all-to-all-start.4
  291.6 6.7 all-reduce.4
  301.8 10.7 %all-to-all-done.4 = bf16[8,72,768]{2,1,0:T(8,128)(2,1)S(1)} async-done(((bf16[8,72,768]{2,1,0:T(8,128)(2,1)}), bf16[8,72,768]{2,1,0:T(8,128)(2,1)S(1)}, u32[]{:S(2)}, u32[]{:S(2)}) %all-to-all-start.4) | async-done | bytes 884768 | tf_op jit(solution)/shard_map/all_to_all | solution.py:179
  314.0 10.8 %fusion.64 = bf16[1200,768]{1,0:T(8,128)(2,1)S(1)} fusion(bf16[1200,3072]{1,0:T(8,128)(2,1)} %copy-done.72, bf16[3072,768]{1,0:T(8,128)(2,1)} %all-gather.8.cloned.1.call-done, f32[768]{0:T(1024)S(1)} %all-reduce.4, f32[1200,768]{1,0:T(8,128)} %copy-done.1, bf16[576,768]{1,0:T(8,128)(2,1)S(1)} %bitcast.201, f32[1200]{0:T(1024)S(1)} %fusion.123), kind=kOutput, calls=%fused_computation.99 | convolution fusion | flops 5667840000 | bytes 18513600 | tf_op jit(solution)/shard_map/dot_general | solution.py:37
  324.9 7.6 %collective-permute-done.3 = bf16[576,768]{1,0:T(8,128)(2,1)S(1)} collective-permute-done((bf16[576,768]{1,0:T(8,128)(2,1)S(1)}, bf16[576,768]{1,0:T(8,128)(2,1)S(1)}, u32[]{:S(2)}, u32[]{:S(2)}) %collective-permute-start.3) | collective-permute-done | bytes 884768 | tf_op jit(solution)/shard_map/ppermute | solution.py:230
  334.0 10.3 %convolution_convert_fusion.1 = bf16[768,3072]{1,0:T(8,128)(2,1)S(1)} fusion(bf16[1200,3072]{1,0:T(8,128)(2,1)} %copy-done.71, f32[768]{0:T(1024)S(1)} %get-tuple-element.24, f32[768]{0:T(1024)S(1)} %get-tuple-element.23, f32[1200]{0:T(1024)S(1)} %add_rsqrt_fusion, f32[1200]{0:T(1024)S(1)} %broadcast_multiply_fusion.2, f32[1200,768]{1,0:T(8,128)S(1)} %copy-done.4, ...), kind=kOutput, calls=%fused_computation.66 | convolution fusion | flops 5672042496 | bytes 16683072 | tf_op jit(solution)/shard_map/dot_general | solution.py:41
  344.3 2.5 copy.186
  349.5 3.6 all-to-all-start.2
  353.7 7.9 %fusion.56 = bf16[2432,192]{0,1:T(8,128)(2,1)} fusion(s32[2304]{0:T(1024)S(1)} %copy-done.51, s32[2432]{0:T(1024)S(1)} %copy-done.55, bf16[192,768]{1,0:T(8,128)(2,1)S(1)} %copy-done.28, bf16[1152,768]{1,0:T(8,128)(2,1)} %collective-permute-done.4, bf16[576,768]{1,0:T(8,128)(2,1)} %copy-done.25, bf16[576,768]{1,0:T(8,128)(2,1)S(1)} %bitcast.214), kind=kOutput, calls=%fused_computation.81 | convolution fusion | flops 2848284672 | bytes 4786688 | tf_op jit(solution)/shard_map/dot_general | solution.py:37
  361.6 3.8 reshape.354
  365.5 8.5 %fusion.75 = bf16[8,304,1,3,64]{1,4,3,0,2:T(8,128)(2,1)} fusion(bf16[8,304,3,64]{1,0,3,2:T(8,128)(2,1)} %reshape.354, f32[8,3,304,304]{2,3,1,0:T(8,128)} %get-tuple-element.66, f32[8,3,304]{2,1,0:T(4,128)} %copy-done.35), kind=kOutput, calls=%fused_computation.130 | convolution fusion | flops 288337920 | bytes 10768896 | tf_op jit(solution)/shard_map/rhqk,rqhe->rkhe/dot_general | solution.py:236
  374.0 7.5 %multiply_reduce_fusion = (f32[8,3,304]{2,1,0:T(4,128)S(1)}, f32[8,3,304,304]{2,3,1,0:T(8,128)S(1)}) fusion(f32[8,3,304,304]{2,3,1,0:T(8,128)} %get-tuple-element.66, f32[8,3,304]{2,1,0:T(4,128)S(1)} %copy-done.36, bf16[8,304,1,3,64]{1,0,4,3,2:T(8,128)(2,1)S(1)} %copy-done.21, bf16[8,304,3,64]{1,0,3,2:T(8,128)(2,1)} %reshape.354), kind=kOutput, calls=%fused_computation.40 | convolution fusion | flops 290548608 | bytes 19670016 | tf_op jit(solution)/shard_map/rqhe,rkhe->rhqk/dot_general | solution.py:235
  387.5 4.1 copy.131
  391.6 6.5 convert_element_type.200
  398.1 4.4 all-to-all-start.3
  402.6 16.6 %fusion.62 = f32[2304,768]{1,0:T(8,128)} fusion(bf16[768,576]{0,1:T(8,128)(2,1)S(1)} %bitcast.192, bf16[2432,576]{0,1:T(8,128)(2,1)} %convert_element_type.200, s32[2304]{0:T(1024)S(1)} %copy-done.52, s32[2432]{0:T(1024)S(1)} %copy-done.56), kind=kOutput, calls=%fused_computation.98 | convolution fusion | flops 8500396032 | bytes 10783232 | tf_op jit(solution)/shard_map/dot_general | solution.py:45
  419.2 3.6 slice.288
  427.9 2.4 multiply_reduce_fusion.1
  435.1 3.5 all-to-all-start.7
  442.3 13.4 %fusion.2 = f32[4616,192]{0,1:T(8,128)} fusion(bf16[2496,192]{0,1:T(8,128)(2,1)} %reshape.351, s32[4616]{0:T(1024)S(1)} %copy-done.41), kind=kOutput, calls=%fused_computation.3 | convolution fusion | flops 4435791360 | bytes 4522016 | tf_op jit(solution)/shard_map/dot_general | solution.py:37
  455.7 3.0 slice_add_fusion
  463.6 12.8 %fusion.40 = bf16[4616,192]{0,1:T(8,128)(2,1)} fusion(f32[4616,192]{0,1:T(8,128)S(1)} %copy-done.73, bf16[2304,192]{0,1:T(8,128)(2,1)S(1)} %copy-done.27, s32[4616]{0:T(1024)S(1)} %copy-done.39), kind=kOutput, calls=%fused_computation.57 | convolution fusion | flops 4096349184 | bytes 6220832 | tf_op jit(solution)/shard_map/dot_general | solution.py:37
  478.9 5.0 collective-permute-done.6
  483.9 2.8 fusion.71
  486.7 5.3 all-to-all-start.5
  494.1 6.3 convolution_convert_fusion.3
  502.0 3.1 fusion.86
  506.9 4.6 collective-permute-start.9
  511.5 2.8 all-to-all-done.5
  516.2 2.7 fusion.74
  518.9 3.0 add_convert_fusion.3
  523.3 3.7 all-to-all-start.6
  527.1 13.4 %fusion.1 = f32[4616,192]{0,1:T(8,128)} fusion(bf16[2496,192]{0,1:T(8,128)(2,1)} %reshape.359, s32[4616]{0:T(1024)S(1)} %copy-done.42), kind=kOutput, calls=%fused_computation.2 | convolution fusion | flops 4435791360 | bytes 4522016 | tf_op jit(solution)/shard_map/dot_general | solution.py:37
  541.9 40.4 %psum.37 = f32[11,768]{1,0:T(8,128)S(1)} all-reduce(f32[11,768]{1,0:T(8,128)S(1)} %concatenate.16), channel_id=1, replica_groups=mesh['tok'=8,'tp'=4] {'tok','tp'}, use_global_device_ids=true, to_apply=%region_31.32 | all-reduce | flops 8448 | bytes 67584 | tf_op jit(solution)/shard_map/psum | solution.py:274
  585.7 13.6 %fusion.39 = f32[4616,192]{0,1:T(8,128)} fusion(f32[4616,192]{0,1:T(8,128)} %fusion.1, bf16[2304,192]{0,1:T(8,128)(2,1)S(1)} %reshape.357, s32[4616]{0:T(1024)S(1)} %copy-done.40), kind=kOutput, calls=%fused_computation.56 | convolution fusion | flops 4095462912 | bytes 7993376 | tf_op jit(solution)/shard_map/dot_general | solution.py:37
  599.3 56.6 %all-reduce.8.cloned.1.call-done = (bf16[768,3,192]{0,2,1:T(8,128)(2,1)}, bf16[192,768]{1,0:T(8,128)(2,1)}, bf16[768,768]{1,0:T(8,128)(2,1)}, bf16[768,768]{1,0:T(8,128)(2,1)}) async-done(((bf16[768,3,192]{0,2,1:T(8,128)(2,1)}, bf16[192,768]{1,0:T(8,128)(2,1)}, bf16[768,768]{1,0:T(8,128)(2,1)}, bf16[768,768]{1,0:T(8,128)(2,1)}), (bf16[768,3,192]{0,2,1:T(8,128)(2,1)}, bf16[192,768]{1,0:T(8,128)(2,1)}, ...) | async-done | bytes 3538960 | tf_op jit(solution)/shard_map/psum | solution.py:250
  657.9 2.5 reshape.361
  (317 shorter events, 85.0 us)
Async XLA Ops:
  7.2 99.3 %copy-start = (bf16[768,3,192]{0,2,1:T(8,128)(2,1)S(1)}, bf16[768,3,192]{0,2,1:T(8,128)(2,1)}, u32[]{:S(2)}) copy-start(bf16[768,3,192]{0,2,1:T(8,128)(2,1)} %param.20) | copy-start | bytes 2654212
  7.2 211.3 %all-gather.6.cloned.1.call-start = ((), (), s32[]{:S(2)}) async-start(), calls=%async_computation.12 | async-start | bytes 5898240 | tf_op jit(solution)/shard_map/all_gather | solution.py:112
  8.1 23.2 %copy-start.29 = (f32[768]{0:T(1024)}, f32[768]{0:T(1024)S(1)}, u32[]{:S(2)}) copy-start(f32[768]{0:T(1024)S(1)} %get-tuple-element.21) | copy-start | bytes 9220
  32.1 49.2 %copy-start.68 = (f32[192]{0:T(256)S(1)}, f32[192]{0:T(256)}, u32[]{:S(2)}) copy-start(f32[192]{0:T(256)} %param.23) | copy-start | bytes 2308
  32.1 49.4 %copy-start.67 = (f32[2,192]{1,0:T(2,128)S(1)}, f32[2,192]{1,0:T(2,128)}, u32[]{:S(2)}) copy-start(f32[2,192]{1,0:T(2,128)} %param.21) | copy-start | bytes 4612
  80.6 3.9 collective-permute-start
  80.7 169.3 %all-gather.8.cloned.1.call-start = ((), (), s32[]{:S(2)}) async-start(), calls=%async_computation.13 | async-start | bytes 5898240 | tf_op jit(solution)/shard_map/all_gather | solution.py:113
  81.6 21.0 %copy-start.53 = (s32[2432]{0:T(1024)}, s32[2432]{0:T(1024)S(1)}, u32[]{:S(2)}) copy-start(s32[2432]{0:T(1024)S(1)} %fusion.120) | copy-start | bytes 29188
  89.7 51.7 %copy-start.50 = (s32[2304]{0:T(1024)}, s32[2304]{0:T(1024)S(1)}, u32[]{:S(2)}) copy-start(s32[2304]{0:T(1024)S(1)} %eq.201) | copy-start | bytes 27652
  149.7 3.9 collective-permute-start.1
  149.9 8.5 %copy-start.43 = (s32[4616]{0:T(1024)S(1)}, s32[4616]{0:T(1024)}, u32[]{:S(2)}) copy-start(s32[4616]{0:T(1024)} %get-tuple-element.47) | copy-start | bytes 55396
  157.0 41.9 %collective-permute-start.2 = (bf16[576,768]{1,0:T(8,128)(2,1)S(1)}, bf16[576,768]{1,0:T(8,128)(2,1)S(1)}, u32[]{:S(2)}, u32[]{:S(2)}) collective-permute-start(bf16[576,768]{1,0:T(8,128)(2,1)S(1)} %slice.292), channel_id=1, source_target_pairs={{0,2},{1,3},{2,0},{3,1},{4,6},{5,7},{6,4},{7,5},{8,10},{9,11},{10,... | collective-permute-start | bytes 2654216 | tf_op jit(solution)/shard_map/ppermute | solution.py:175
  158.4 15.2 %copy-start.64 = (f32[768]{0:T(1024)S(1)}, f32[768]{0:T(1024)}, u32[]{:S(2)}) copy-start(f32[768]{0:T(1024)} %param.26) | copy-start | bytes 9220
  158.4 15.2 %copy-start.44 = (f32[768]{0:T(1024)S(1)}, f32[768]{0:T(1024)}, u32[]{:S(2)}) copy-start(f32[768]{0:T(1024)} %param.18) | copy-start | bytes 9220
  173.5 25.4 %copy-start.63 = (f32[2,768]{1,0:T(2,128)S(1)}, f32[2,768]{1,0:T(2,128)}, u32[]{:S(2)}) copy-start(f32[2,768]{1,0:T(2,128)} %param.24) | copy-start | bytes 18436
  178.6 39.8 %copy-start.31 = (f32[1200]{0:T(1024)}, f32[1200]{0:T(1024)S(1)}, u32[]{:S(2)}) copy-start(f32[1200]{0:T(1024)S(1)} %convolution_reduce_fusion) | copy-start | bytes 14404
  200.0 26.5 %all-to-all-start.1 = ((bf16[8,72,768]{2,1,0:T(8,128)(2,1)}), bf16[8,72,768]{2,1,0:T(8,128)(2,1)S(1)}, u32[]{:S(2)}, u32[]{:S(2)}) async-start(bf16[8,72,768]{2,1,0:T(8,128)(2,1)} %bitcast.21), calls=%async_computation.1 | async-start | bytes 1769472 | tf_op jit(solution)/shard_map/all_to_all | solution.py:179
  203.6 312.5 %reduce-scatter.5.cloned.1.call-start = ((), (), s32[]{:S(2)}) async-start(), calls=%async_computation.11 | async-start | bytes 5898240 | tf_op jit(solution)/shard_map/reduce_scatter | solution.py:226
  231.1 10.5 %copy-start.19 = (bf16[1200,768]{1,0:T(8,128)(2,1)S(1)}, bf16[1200,768]{1,0:T(8,128)(2,1)}, u32[]{:S(2)}) copy-start(bf16[1200,768]{1,0:T(8,128)(2,1)} %fusion.65) | copy-start | bytes 5529604
  250.0 14.4 %copy-start.3 = (f32[1200,768]{1,0:T(8,128)S(1)}, f32[1200,768]{1,0:T(8,128)}, u32[]{:S(2)}) copy-start(f32[1200,768]{1,0:T(8,128)} %copy-done.1) | copy-start | bytes 11059204
  264.3 13.4 %copy-start.71 = (bf16[1200,3072]{1,0:T(8,128)(2,1)}, bf16[1200,3072]{1,0:T(8,128)(2,1)S(1)}, u32[]{:S(2)}) copy-start(bf16[1200,3072]{1,0:T(8,128)(2,1)S(1)} %get-tuple-element.73) | copy-start | bytes 22118404
  264.3 13.4 %copy-start.20 = (bf16[1200,768]{1,0:T(8,128)(2,1)S(1)}, bf16[1200,768]{1,0:T(8,128)(2,1)}, u32[]{:S(2)}) copy-start(bf16[1200,768]{1,0:T(8,128)(2,1)} %fusion.65) | copy-start | bytes 5529604
  281.9 9.5 %copy-start.69 = (f32[192]{0:T(256)S(1)}, f32[192]{0:T(256)}, u32[]{:S(2)}) copy-start(f32[192]{0:T(256)} %param.28) | copy-start | bytes 2308
  285.4 27.0 %all-to-all-start.4 = ((bf16[8,72,768]{2,1,0:T(8,128)(2,1)}), bf16[8,72,768]{2,1,0:T(8,128)(2,1)S(1)}, u32[]{:S(2)}, u32[]{:S(2)}) async-start(bf16[8,72,768]{2,1,0:T(8,128)(2,1)} %bitcast.32), calls=%async_computation.4 | async-start | bytes 1769472 | tf_op jit(solution)/shard_map/all_to_all | solution.py:179
  312.4 20.0 %copy-start.14 = (bf16[8,72,768]{2,1,0:T(8,128)(2,1)}, bf16[8,72,768]{2,1,0:T(8,128)(2,1)S(1)}, u32[]{:S(2)}) copy-start(bf16[8,72,768]{2,1,0:T(8,128)(2,1)S(1)} %all-to-all-done.4) | copy-start | bytes 2654212
  312.5 20.0 %collective-permute-start.3 = (bf16[576,768]{1,0:T(8,128)(2,1)S(1)}, bf16[576,768]{1,0:T(8,128)(2,1)S(1)}, u32[]{:S(2)}, u32[]{:S(2)}) collective-permute-start(bf16[576,768]{1,0:T(8,128)(2,1)S(1)} %bitcast.212), channel_id=1, source_target_pairs={{0,2},{1,3},{2,0},{3,1},{4,6},{5,7},{6,4},{7,5},{8,10},{9,11},{10,... | collective-permute-start | bytes 2654216 | tf_op jit(solution)/shard_map/ppermute | solution.py:230
  324.8 9.0 %copy-start.13 = (bf16[1200,768]{1,0:T(8,128)(2,1)}, bf16[1200,768]{1,0:T(8,128)(2,1)S(1)}, u32[]{:S(2)}) copy-start(bf16[1200,768]{1,0:T(8,128)(2,1)S(1)} %fusion.64) | copy-start | bytes 5529604
  324.8 9.1 %copy-start.4 = (f32[1200,768]{1,0:T(8,128)S(1)}, f32[1200,768]{1,0:T(8,128)}, u32[]{:S(2)}) copy-start(f32[1200,768]{1,0:T(8,128)} %copy-done.1) | copy-start | bytes 11059204
  334.0 19.7 %collective-permute-start.4 = (bf16[1152,768]{1,0:T(8,128)(2,1)}, bf16[1152,768]{1,0:T(8,128)(2,1)}, u32[]{:S(2)}, u32[]{:S(2)}) collective-permute-start(bf16[1152,768]{1,0:T(8,128)(2,1)} %pad_maximum_fusion.2), channel_id=1, source_target_pairs={{0,1},{1,0},{2,3},{3,2},{4,5},{5,4},{6,7},{7,6},{8,9},{9,8},{10,11... | collective-permute-start | bytes 5308424 | tf_op jit(solution)/shard_map/ppermute | solution.py:231
  349.5 48.7 %all-to-all-start.2 = ((bf16[4,576,192]{1,2,0:T(8,128)(2,1)}), bf16[4,576,192]{1,2,0:T(8,128)(2,1)S(1)}, u32[]{:S(2)}, u32[]{:S(2)}) async-start(bf16[4,576,192]{1,2,0:T(8,128)(2,1)} %bitcast.29), calls=%async_computation.2 | async-start | bytes 1966080 | tf_op jit(solution)/shard_map/all_to_all | solution.py:262
  353.1 163.0 %reduce-scatter.3.cloned.1.call-start = ((), (), s32[]{:S(2)}) async-start(), calls=%async_computation.10 | async-start | bytes 5898240 | tf_op jit(solution)/shard_map/reduce_scatter | solution.py:225
  365.5 8.5 %copy-start.21 = (bf16[8,304,1,3,64]{1,0,4,3,2:T(8,128)(2,1)S(1)}, bf16[8,304,1,3,64]{1,0,4,3,2:T(8,128)(2,1)}, u32[]{:S(2)}) copy-start(bf16[8,304,1,3,64]{1,0,4,3,2:T(8,128)(2,1)} %get-tuple-element.39) | copy-start | bytes 2801668
  365.5 8.5 %copy-start.36 = (f32[8,3,304]{2,1,0:T(4,128)S(1)}, f32[8,3,304]{2,1,0:T(4,128)}, u32[]{:S(2)}) copy-start(f32[8,3,304]{2,1,0:T(4,128)} %copy-done.35) | copy-start | bytes 87556
  365.5 16.0 %slice-start = ((s8[11206656]{0:T(1024)(128)(4,1)}), s8[4194304]{0:T(1024)(128)(4,1)S(1)}, s32[]{:S(2)}) async-start(s8[11206656]{0:T(1024)(128)(4,1)} %bitcast.203), calls=%async_computation.15 | async-start | bytes 8388608
  365.5 16.0 %slice-start.1 = ((s8[11206656]{0:T(1024)(128)(4,1)}), s8[4194304]{0:T(1024)(128)(4,1)S(1)}, s32[]{:S(2)}) async-start(s8[11206656]{0:T(1024)(128)(4,1)} %bitcast.203), calls=%async_computation.16 | async-start | bytes 8388608
  391.6 11.0 %copy-start.52 = (s32[2304]{0:T(1024)S(1)}, s32[2304]{0:T(1024)}, u32[]{:S(2)}) copy-start(s32[2304]{0:T(1024)} %copy-done.50) | copy-start | bytes 27652
  391.6 11.0 %copy-start.56 = (s32[2432]{0:T(1024)S(1)}, s32[2432]{0:T(1024)}, u32[]{:S(2)}) copy-start(s32[2432]{0:T(1024)} %copy-done.53) | copy-start | bytes 29188
  398.1 37.0 %all-to-all-start.3 = ((bf16[4,624,192]{1,2,0:T(8,128)(2,1)}), bf16[4,624,192]{1,2,0:T(8,128)(2,1)}, u32[]{:S(2)}, u32[]{:S(2)}) async-start(bf16[4,624,192]{1,2,0:T(8,128)(2,1)} %bitcast.31), calls=%async_computation.3 | async-start | bytes 1966080 | tf_op jit(solution)/shard_map/all_to_all | solution.py:262
  419.1 8.7 %copy-start.32 = (f32[1200]{0:T(1024)S(1)}, f32[1200]{0:T(1024)}, u32[]{:S(2)}) copy-start(f32[1200]{0:T(1024)} %copy-done.31) | copy-start | bytes 14404
  419.1 8.7 %copy-start.38 = (f32[1200]{0:T(1024)S(1)}, f32[1200]{0:T(1024)}, u32[]{:S(2)}) copy-start(f32[1200]{0:T(1024)} %get-tuple-element.33) | copy-start | bytes 14404
  422.8 33.0 %collective-permute-start.5 = (bf16[1152,768]{1,0:T(8,128)(2,1)}, bf16[1152,768]{1,0:T(8,128)(2,1)}, u32[]{:S(2)}, u32[]{:S(2)}) collective-permute-start(bf16[1152,768]{1,0:T(8,128)(2,1)} %slice.288), channel_id=1, source_target_pairs={{0,1},{1,0},{2,3},{3,2},{4,5},{5,4},{6,7},{7,6},{8,9},{9,8},{10,11... | collective-permute-start | bytes 5308424 | tf_op jit(solution)/shard_map/ppermute | solution.py:173
  433.5 8.8 %copy-start.41 = (s32[4616]{0:T(1024)S(1)}, s32[4616]{0:T(1024)}, u32[]{:S(2)}) copy-start(s32[4616]{0:T(1024)} %get-tuple-element.49) | copy-start | bytes 55396
  435.1 41.2 %all-to-all-start.7 = ((bf16[4,624,192]{1,2,0:T(8,128)(2,1)}), bf16[4,624,192]{1,2,0:T(8,128)(2,1)S(1)}, u32[]{:S(2)}, u32[]{:S(2)}) async-start(bf16[4,624,192]{1,2,0:T(8,128)(2,1)} %bitcast.211), calls=%async_computation.7 | async-start | bytes 1966080 | tf_op jit(solution)/shard_map/all_to_all | solution.py:262
  461.6 22.3 %collective-permute-start.6 = (bf16[576,768]{1,0:T(8,128)(2,1)}, bf16[576,768]{1,0:T(8,128)(2,1)}, u32[]{:S(2)}, u32[]{:S(2)}) collective-permute-start(bf16[576,768]{1,0:T(8,128)(2,1)} %slice.291), channel_id=1, source_target_pairs={{0,2},{1,3},{2,0},{3,1},{4,6},{5,7},{6,4},{7,5},{8,10},{9,11},{10,... | collective-permute-start | bytes 2654216 | tf_op jit(solution)/shard_map/ppermute | solution.py:175
  486.7 27.7 %all-to-all-start.5 = ((bf16[8,72,768]{2,1,0:T(8,128)(2,1)}), bf16[8,72,768]{2,1,0:T(8,128)(2,1)S(1)}, u32[]{:S(2)}, u32[]{:S(2)}) async-start(bf16[8,72,768]{2,1,0:T(8,128)(2,1)} %bitcast.40), calls=%async_computation.5 | async-start | bytes 1769472 | tf_op jit(solution)/shard_map/all_to_all | solution.py:179
  492.0 163.9 %all-reduce.8.cloned.1.call-start = ((), (), s32[]{:S(2)}) async-start(), calls=%async_computation.14 | async-start | bytes 7077888 | tf_op jit(solution)/shard_map/psum | solution.py:250
  492.1 9.9 %copy-start.16 = (bf16[8,72,768]{2,1,0:T(8,128)(2,1)S(1)}, bf16[8,72,768]{2,1,0:T(8,128)(2,1)}, u32[]{:S(2)}) copy-start(bf16[8,72,768]{2,1,0:T(8,128)(2,1)} %copy-done.14) | copy-start | bytes 2654212
  492.1 9.9 %copy-start.18 = (bf16[2304,192]{0,1:T(8,128)(2,1)S(1)}, bf16[2304,192]{0,1:T(8,128)(2,1)}, u32[]{:S(2)}) copy-start(bf16[2304,192]{0,1:T(8,128)(2,1)} %copy-done.17) | copy-start | bytes 2654212
  492.1 9.9 %copy-start.26 = (bf16[576,768]{1,0:T(8,128)(2,1)S(1)}, bf16[576,768]{1,0:T(8,128)(2,1)}, u32[]{:S(2)}) copy-start(bf16[576,768]{1,0:T(8,128)(2,1)} %copy-done.25) | copy-start | bytes 2654212
  492.1 8.3 %collective-permute-start.7 = (f32[2,192]{1,0:T(2,128)S(1)}, f32[2,192]{1,0:T(2,128)S(1)}, u32[]{:S(2)}, u32[]{:S(2)}) collective-permute-start(f32[2,192]{1,0:T(2,128)S(1)} %pad_maximum_fusion.8), channel_id=1, source_target_pairs={{0,4},{4,0},{8,12},{12,8},{16,20},{20,16},{24,28},{28,24},{1,5},{5... | collective-permute-start | bytes 4616 | tf_op jit(solution)/shard_map/ppermute | solution.py:283
  500.4 13.9 %copy-start.30 = (f32[768]{0:T(1024)S(1)}, f32[768]{0:T(1024)}, u32[]{:S(2)}) copy-start(f32[768]{0:T(1024)} %copy-done.29) | copy-start | bytes 9220
  500.4 5.9 collective-permute-start.8
  505.0 11.1 %copy-start.37 = (f32[576]{0:T(1024)S(1)}, f32[576]{0:T(1024)}, u32[]{:S(2)}) copy-start(f32[576]{0:T(1024)} %add_rsqrt_fusion.2) | copy-start | bytes 6916
  506.9 33.6 %collective-permute-start.9 = (f32[2,192]{1,0:T(2,128)}, f32[2,192]{1,0:T(2,128)}, u32[]{:S(2)}, u32[]{:S(2)}) collective-permute-start(f32[2,192]{1,0:T(2,128)} %fusion.173), channel_id=1, source_target_pairs={{0,16},{4,20},{8,24},{12,28},{16,0},{20,4},{24,8},{28,12},{1,17},{... | collective-permute-start | bytes 4616 | tf_op jit(solution)/shard_map/ppermute | solution.py:283
  523.3 61.0 %all-to-all-start.6 = ((bf16[4,576,192]{1,2,0:T(8,128)(2,1)}), bf16[4,576,192]{1,2,0:T(8,128)(2,1)S(1)}, u32[]{:S(2)}, u32[]{:S(2)}) async-start(bf16[4,576,192]{1,2,0:T(8,128)(2,1)} %bitcast.43), calls=%async_computation.6 | async-start | bytes 1966080 | tf_op jit(solution)/shard_map/all_to_all | solution.py:262
  527.0 14.8 %copy-start.47 = (f32[768]{0:T(1024)S(1)}, f32[768]{0:T(1024)}, u32[]{:S(2)}) copy-start(f32[768]{0:T(1024)} %get-tuple-element.19) | copy-start | bytes 9220
  527.0 14.8 %copy-start.49 = (f32[768]{0:T(1024)S(1)}, f32[768]{0:T(1024)}, u32[]{:S(2)}) copy-start(f32[768]{0:T(1024)} %get-tuple-element.15) | copy-start | bytes 9220
  527.0 14.8 %copy-start.34 = (f32[4,768]{1,0:T(4,128)S(1)}, f32[4,768]{1,0:T(4,128)}, u32[]{:S(2)}) copy-start(f32[4,768]{1,0:T(4,128)} %reshape.362) | copy-start | bytes 36868
  527.0 14.8 %copy-start.58 = (f32[1,768]{1,0:T(1,128)S(1)}, f32[1,768]{1,0:T(1,128)}, u32[]{:S(2)}) copy-start(f32[1,768]{1,0:T(1,128)} %stack.69) | copy-start | bytes 9220
  527.0 14.8 %copy-start.59 = (f32[1,768]{1,0:T(1,128)S(1)}, f32[1,768]{1,0:T(1,128)}, u32[]{:S(2)}) copy-start(f32[1,768]{1,0:T(1,128)} %stack.70) | copy-start | bytes 9220
  527.0 14.8 %copy-start.60 = (f32[1,768]{1,0:T(1,128)S(1)}, f32[1,768]{1,0:T(1,128)}, u32[]{:S(2)}) copy-start(f32[1,768]{1,0:T(1,128)} %stack.71) | copy-start | bytes 9220
  527.0 14.8 %copy-start.61 = (f32[1,768]{1,0:T(1,128)S(1)}, f32[1,768]{1,0:T(1,128)}, u32[]{:S(2)}) copy-start(f32[1,768]{1,0:T(1,128)} %stack.73) | copy-start | bytes 9220
  527.0 14.8 %copy-start.62 = (f32[1,768]{1,0:T(1,128)S(1)}, f32[1,768]{1,0:T(1,128)}, u32[]{:S(2)}) copy-start(f32[1,768]{1,0:T(1,128)} %stack.72) | copy-start | bytes 9220
  540.5 45.2 %copy-start.40 = (s32[4616]{0:T(1024)S(1)}, s32[4616]{0:T(1024)}, u32[]{:S(2)}) copy-start(s32[4616]{0:T(1024)} %get-tuple-element.45) | copy-start | bytes 55396
  (38 other events, 179.9 us)
Sparse Core Ops, SparseCore 0:
  80.8 36.5 all-gather.5
  150.0 55.4 all-gather.7
  250.0 47.8 reduce-scatter.4
  356.3 48.7 reduce-scatter.2
  516.3 139.6 all-reduce.7
